TPU v7x, 768 devices: a whole 4x8x12 slice. The times are simulated.
768 devices in a mesh: dom: 96 (over z, y), sub: 8 (over x, core).
Axes of the slice: x: 4, y: 8, z: 12, core: 2. Of those that a mesh axis runs over, the one named last changes fastest.
Arguments:
- modal_state: float32 [56, 9, 98304], P(None, None, ('dom', 'sub')), may hold values from -6 to 6
- cluster_id: int32 [98304], P(('dom', 'sub')), may hold values 0 or 1
- jacobian_id: int32 [98304], P(('dom', 'sub')), may hold values from 0 to 63
- face_neighbour: int32 [4, 98304], P(None, ('dom', 'sub')), may hold values from 0 to 320, as said below
- flux_index: int32 [4, 98304], P(None, ('dom', 'sub')), may hold values from 0 to 11, as said below
- send_list: int32 [147456], P(('dom', 'sub')), may hold values from 0 to 511, as said below
- derivative: float32 [3, 56, 56], replicated, may hold values from -1.25 to 1.25
- stiffness: float32 [3, 56, 56], replicated, may hold values from -0.75 to 0.75
- restriction: float32 [4, 21, 56], replicated, may hold values from -0.75 to 0.75
- lifting: float32 [4, 56, 21], replicated, may hold values from -1.25 to 1.25
- orientation: float32 [3, 21, 21], replicated, may hold values from -1.25 to 1.25
- star_matrix: float32 [64, 3, 9, 9], replicated, may hold values from -2 to 2
- flux_minus: float32 [64, 4, 9, 9], replicated, may hold values from -2 to 2
- flux_plus: float32 [64, 4, 9, 9], replicated, may hold values from -2 to 2
Outputs:
- new_state: float32 [56, 9, 98304], P(None, None, ('dom', 'sub'))
Inputs may be any that keep to these rules, and one draw needn't show every extreme that they name: `face_neighbour`: each device's 4 * 128 faces are all distinct between interior pairs, live ghost slots and faces without neighbour. Along dom the devices at both ends have empty outer blocks; some device fills a dom block of 64 slots and every dom group has two sub-blocks sharing 8 faces. For a face whose neighbour is in a ghost slot, flux_index // 3 equals the face number listed in the sender's send_list slot divided by 128. `send_list`: the first 192 faces of a permutation of each device's 4 * 128 faces; slots past a link's count list faces without a neighbour.
All inputs are finite; a program needn't handle non-finite values. No bound on the sum of `cluster_id` on one device may be relied on, other than what follows from the above.
Results may differ from a plain program's by a relative error of at most 0.0003.
Values sent between devices are 32-bit elements; how exact they have to be, the bound alone decides.
A program may use at most 64 MiB of HBM per device.

v0:
```python
import functools
import math

import jax
import jax.numpy as jnp
from jax import lax
from jax.experimental import pallas as pl
from jax.experimental.pallas import tpu as pltpu
from jax.sharding import PartitionSpec as P

ORDER = 6
CAP_DOM = 64
CAP_SUB = 8
VARS = 9
BASIS = 56
FACE = 21
FPAD = 24
LANES = 128
CLASSES = 64
GHOSTS = 192
PAIRS = VARS * VARS
KDIM = 176
WIDE = 256
F32 = jnp.float32
BF16 = jnp.bfloat16
MESH = pl.DeviceIdType.MESH

half = 0.5
half_weights = [half ** (k + 1) / math.factorial(k + 1) for k in range(ORDER)]
late_weights = [(1.0 - half ** (k + 1)) / math.factorial(k + 1) for k in range(ORDER)]


def split(values):
    high = values.astype(BF16).astype(F32)
    return high, values - high


def left_operand(matrix, pad):
    high, low = split(matrix)
    parts = [high, low, high]
    if pad:
        parts.append(jnp.zeros((matrix.shape[0], pad), F32))
    return jnp.concatenate(parts, axis=1).astype(BF16)


def right_operand(values, pad):
    high, low = split(values)
    parts = [high, high, low]
    if pad:
        parts.append(jnp.zeros((pad, values.shape[1]), F32))
    return jnp.concatenate(parts, axis=0).astype(BF16)


def dot(left, right):
    return jnp.dot(left, right, preferred_element_type=F32)


def lookup(table, onehot):
    high, low = split(table)
    return dot(high.astype(BF16), onehot) + dot(low.astype(BF16), onehot)


def kernel(
    n_dom,
    n_sub,
    state,
    cluster,
    jacobian,
    neighbour,
    flux,
    send,
    derivative,
    stiffness,
    restriction,
    lifting,
    orientation,
    star,
    minus,
    plus,
    out,
    star_rows,
    minus_rows,
    plus_rows,
    left_derivative,
    left_stiffness,
    left_restriction,
    left_lifting,
    left_orientation,
    faces,
    turns,
    pick_send,
    pick_local,
    pick_ghost,
    current,
    moved,
    half_sum,
    late_sum,
    own,
    candidates,
    gathered,
    lift_in,
    payload,
    received,
    send_sem,
    recv_sem,
):
    dom = lax.axis_index("dom")
    sub = lax.axis_index("sub")
    lower = lax.rem(dom + n_dom - 1, n_dom)
    upper = lax.rem(dom + 1, n_dom)
    peers = [(lower, sub), (upper, sub)]
    peers += [(dom, lax.rem(sub + i, n_sub)) for i in range(1, n_sub)]
    barrier = pltpu.get_barrier_semaphore()
    for peer in peers:
        pl.semaphore_signal(barrier, inc=1, device_id=peer, device_id_type=MESH)

    class_id = lax.broadcasted_iota(jnp.int32, (CLASSES, LANES), 0)
    onehot = (class_id == jacobian[...]).astype(F32).astype(BF16)
    for d in range(3):
        star_rows[pl.ds(d * 88, PAIRS), :] = lookup(star[:, d, :], onehot)
    for f in range(4):
        minus_rows[pl.ds(f * 88, PAIRS), :] = lookup(minus[:, f, :], onehot)
        plus_rows[pl.ds(f * 88, PAIRS), :] = lookup(plus[:, f, :], onehot)

    for d in range(3):
        left_derivative[pl.ds(d * BASIS, BASIS), :] = left_operand(-derivative[d], 8)
        left_stiffness[pl.ds(d * BASIS, BASIS), :] = left_operand(stiffness[d], 8)
    faces[...] = jnp.zeros_like(faces)
    for f in range(4):
        faces[pl.ds(f * FPAD, FACE), :] = restriction[:, f, :]
    left_restriction[...] = left_operand(faces[...], 8)
    for f in range(4):
        faces[pl.ds(f * FPAD, FACE), :] = lifting[:, f, :]
    left_lifting[...] = left_operand(jnp.transpose(faces[...]), 0)
    turns[...] = jnp.zeros_like(turns)
    for h in range(3):
        turns[pl.ds(h * FPAD, FACE), pl.ds(0, FACE)] = orientation[h]
    left_orientation[...] = left_operand(turns[...], 0)

    def same(rows, target):
        index = lax.broadcasted_iota(jnp.int32, (rows, LANES), 0)
        return (index == target).astype(F32).astype(BF16)

    for f in range(4):
        code = neighbour[pl.ds(f, 1), :]
        face = flux[pl.ds(f, 1), :] // 3
        inner = jnp.where(code < LANES, face * LANES + code, -1)
        outer = code - LANES
        pick_local[:, pl.ds(f * LANES, LANES)] = same(4 * LANES, inner)
        pick_ghost[:, pl.ds(f * LANES, LANES)] = same(GHOSTS, outer)
    send_column = jnp.transpose(jnp.broadcast_to(send[...], (8, GHOSTS)))[:, :1]
    lane = lax.broadcasted_iota(jnp.int32, (GHOSTS, 4 * LANES), 1)
    pick_send[...] = (lane == send_column).astype(F32).astype(BF16)
    candidates[...] = jnp.zeros_like(candidates)
    out[...] = state[...]

    def mix(left, rows, emit):
        moved[...] = dot(left[...], current[...])
        for first_var in range(0, VARS, 3):
            totals = [None] * 3
            for d in range(3):
                for q in range(VARS):
                    block = moved[pl.ds(d * BASIS, BASIS), pl.ds(q * LANES, LANES)]
                    for i in range(3):
                        row = rows[pl.ds(d * 88 + q * VARS + first_var + i, 1), :]
                        term = block * row
                        totals[i] = term if totals[i] is None else totals[i] + term
            for i in range(3):
                emit(first_var + i, totals[i])

    def put(q, values):
        current[:, pl.ds(q * LANES, LANES)] = right_operand(values, 8)

    def weight(table, degree):
        value = jnp.float32(table[ORDER - 1])
        for k in range(ORDER - 2, 0, -1):
            value = jnp.where(degree == k, jnp.float32(table[k]), value)
        return value

    def phase(step, carry):
        for q in range(VARS):
            values = out[q]
            put(q, values)
            half_sum[q] = values * half_weights[0]
            late_sum[step, q] = values * late_weights[0]

        def degree_step(degree, carry):
            for_half = weight(half_weights, degree)
            for_late = weight(late_weights, degree)

            def emit(p, values):
                half_sum[p] += values * for_half
                late_sum[step, p] += values * for_late
                put(p, values)

            mix(left_derivative, star_rows, emit)
            return carry

        lax.fori_loop(1, ORDER, degree_step, 0)

        use_half = jnp.logical_or(cluster[...] == 1, step == 0)
        for q in range(VARS):
            put(q, jnp.where(use_half, half_sum[q], late_sum[0, q]))

        projected = dot(left_restriction[...], current[...])
        for q in range(VARS):
            for f in range(4):
                tile = projected[f * FPAD : (f + 1) * FPAD, q * LANES : (q + 1) * LANES]
                own[pl.ds(q * FPAD, FPAD), pl.ds(f * LANES, LANES)] = tile
        high, low = split(own[...])
        candidates[pl.ds(0, VARS * FPAD), :] = high.astype(BF16)
        candidates[pl.ds(WIDE, VARS * FPAD), :] = low.astype(BF16)

        both = lax.dot_general(
            pick_send[...], candidates[...], (((1,), (1,)), ((), ())), preferred_element_type=F32
        )
        payload[step] = both[:, :WIDE] + both[:, WIDE:]

        @pl.when(step == 0)
        def _():
            pl.semaphore_wait(barrier, len(peers))

        copies = []
        for i, peer in enumerate(peers):
            if i == 0:
                source, target, count = 0, CAP_DOM, CAP_DOM
            elif i == 1:
                source, target, count = CAP_DOM, 0, CAP_DOM
            else:
                source = pl.multiple_of(2 * CAP_DOM + peer[1] * CAP_SUB, CAP_SUB)
                target = pl.multiple_of(2 * CAP_DOM + sub * CAP_SUB, CAP_SUB)
                count = CAP_SUB
            copy = pltpu.make_async_remote_copy(
                src_ref=payload.at[step, pl.ds(source, count), :],
                dst_ref=received.at[step, pl.ds(target, count), :],
                send_sem=send_sem.at[step, i],
                recv_sem=recv_sem.at[step, i],
                device_id=peer,
                device_id_type=MESH,
            )
            copy.start()
            copies.append(copy)
        mine = pl.multiple_of(2 * CAP_DOM + sub * CAP_SUB, CAP_SUB)
        received[step, pl.ds(mine, CAP_SUB), :] = payload[step, pl.ds(mine, CAP_SUB), :]

        def add_volume(p, values):
            out[p] += values

        mix(left_stiffness, star_rows, add_volume)

        gathered[...] = dot(candidates[pl.ds(0, VARS * FPAD), :], pick_local[...]) + dot(
            candidates[pl.ds(WIDE, VARS * FPAD), :], pick_local[...]
        )
        for copy in copies:
            copy.wait()

        ghosts = jnp.transpose(received[step])[: VARS * FPAD]
        high, low = split(ghosts)
        gathered[...] += dot(high.astype(BF16), pick_ghost[...]) + dot(
            low.astype(BF16), pick_ghost[...]
        )
        turn = lax.rem(flux[...], 3)
        for q in range(VARS):
            turned = dot(
                left_orientation[...], right_operand(gathered[pl.ds(q * FPAD, FPAD), :], 0)
            )
            for f in range(4):
                lanes = slice(f * LANES, (f + 1) * LANES)
                which = turn[f : f + 1]
                gathered[pl.ds(q * FPAD, FPAD), pl.ds(f * LANES, LANES)] = jnp.where(
                    which == 0,
                    turned[:FPAD, lanes],
                    jnp.where(which == 1, turned[FPAD : 2 * FPAD, lanes], turned[2 * FPAD :, lanes]),
                )
        for f in range(4):
            lanes = pl.ds(f * LANES, LANES)
            for first_var in range(0, VARS, 3):
                totals = [None] * 3
                for q in range(VARS):
                    mine_side = own[pl.ds(q * FPAD, FPAD), lanes]
                    other_side = gathered[pl.ds(q * FPAD, FPAD), lanes]
                    for i in range(3):
                        row = f * 88 + q * VARS + first_var + i
                        term = (
                            mine_side * minus_rows[pl.ds(row, 1), :]
                            + other_side * plus_rows[pl.ds(row, 1), :]
                        )
                        totals[i] = term if totals[i] is None else totals[i] + term
                for i in range(3):
                    high, low = split(totals[i])
                    columns = pl.ds((first_var + i) * LANES, LANES)
                    lift_in[0, pl.ds(f * FPAD, FPAD), columns] = high
                    lift_in[1, pl.ds(f * FPAD, FPAD), columns] = low
        high, low = lift_in[0].astype(BF16), lift_in[1].astype(BF16)
        right = jnp.concatenate([high, high, low], axis=0)
        lifted = dot(left_lifting[...], right)
        for p in range(VARS):
            out[p] += lifted[:, p * LANES : (p + 1) * LANES]
        return carry

    lax.fori_loop(0, 2, phase, 0)


def body(
    modal_state,
    cluster_id,
    jacobian_id,
    face_neighbour,
    flux_index,
    send_list,
    derivative,
    stiffness,
    restriction,
    lifting,
    orientation,
    star_matrix,
    flux_minus,
    flux_plus,
):
    n_dom, n_sub = lax.axis_size("dom"), lax.axis_size("sub")
    state = jnp.transpose(modal_state, (1, 0, 2))
    star = jnp.transpose(star_matrix, (2, 3, 1, 0)).reshape(PAIRS, 3, CLASSES)
    minus = jnp.transpose(flux_minus, (2, 3, 1, 0)).reshape(PAIRS, 4, CLASSES)
    plus = jnp.transpose(flux_plus, (2, 3, 1, 0)).reshape(PAIRS, 4, CLASSES)
    vmem = pl.BlockSpec(memory_space=pltpu.VMEM)
    n_peers = n_sub + 1
    result = pl.pallas_call(
        functools.partial(kernel, n_dom, n_sub),
        name="elastic_step",
        out_shape=jax.ShapeDtypeStruct((VARS, BASIS, LANES), F32),
        in_specs=[vmem] * 14,
        out_specs=vmem,
        scratch_shapes=[
            pltpu.VMEM((3 * 88, LANES), F32),
            pltpu.VMEM((4 * 88, LANES), F32),
            pltpu.VMEM((4 * 88, LANES), F32),
            pltpu.VMEM((3 * BASIS, KDIM), BF16),
            pltpu.VMEM((3 * BASIS, KDIM), BF16),
            pltpu.VMEM((4 * FPAD, KDIM), BF16),
            pltpu.VMEM((BASIS, 12 * FPAD), BF16),
            pltpu.VMEM((3 * FPAD, 3 * FPAD), BF16),
            pltpu.VMEM((4 * FPAD, BASIS), F32),
            pltpu.VMEM((3 * FPAD, FPAD), F32),
            pltpu.VMEM((GHOSTS, 4 * LANES), BF16),
            pltpu.VMEM((4 * LANES, 4 * LANES), BF16),
            pltpu.VMEM((GHOSTS, 4 * LANES), BF16),
            pltpu.VMEM((KDIM, VARS * LANES), BF16),
            pltpu.VMEM((3 * BASIS, VARS * LANES), F32),
            pltpu.VMEM((VARS, BASIS, LANES), F32),
            pltpu.VMEM((2, VARS, BASIS, LANES), F32),
            pltpu.VMEM((VARS * FPAD, 4 * LANES), F32),
            pltpu.VMEM((2 * WIDE, 4 * LANES), BF16),
            pltpu.VMEM((VARS * FPAD, 4 * LANES), F32),
            pltpu.VMEM((2, 4 * FPAD, VARS * LANES), F32),
            pltpu.VMEM((2, GHOSTS, WIDE), F32),
            pltpu.VMEM((2, GHOSTS, WIDE), F32),
            pltpu.SemaphoreType.DMA((2, n_peers)),
            pltpu.SemaphoreType.DMA((2, n_peers)),
        ],
        compiler_params=pltpu.CompilerParams(
            collective_id=0, has_side_effects=True, vmem_limit_bytes=48 * 1024 * 1024
        ),
    )(
        state,
        cluster_id.reshape(1, LANES),
        jacobian_id.reshape(1, LANES),
        face_neighbour,
        flux_index,
        send_list.reshape(1, GHOSTS),
        derivative,
        stiffness,
        jnp.transpose(restriction, (1, 0, 2)),
        jnp.transpose(lifting, (2, 0, 1)),
        orientation,
        star,
        minus,
        plus,
    )
    return jnp.transpose(result, (1, 0, 2))


def solution(mesh):
    placed = (
        P(None, None, ("dom", "sub")),
        P(("dom", "sub")),
        P(("dom", "sub")),
        P(None, ("dom", "sub")),
        P(None, ("dom", "sub")),
        P(("dom", "sub")),
        P(),
        P(),
        P(),
        P(),
        P(),
        P(),
        P(),
        P(),
    )
    return jax.shard_map(
        body, mesh=mesh, in_specs=placed, out_specs=P(None, None, ("dom", "sub")), check_vma=False
    )
```

profile of v0, /device:TPU:1, one launch (start us, length us, event | category | flops | bytes accessed | tf_op | source)
XLA Modules:
  0.0 48.5 jit_solution(135459166400174513)
XLA Ops:
  0.0 0.0 copy-start.13
  0.0 0.0 copy-start.10
  0.0 0.0 copy-start.9
  0.0 0.0 copy-start.11
  0.0 0.0 copy-start.12
  0.0 0.6 %copy-done.13 = s32[128]{0:T(128)S(1)} copy-done((s32[128]{0:T(128)S(1)}, s32[128]{0:T(128)}, u32[]{:S(2)}) %copy-start.13) | copy-done | bytes 536
  0.7 0.0 copy-done.10
  0.7 0.0 copy-done.9
  0.7 0.0 copy-done.11
  0.7 0.0 copy-done.12
  0.7 0.0 copy-start
  0.7 0.9 %copy-done = f32[56,9,128]{2,0,1:T(8,128)S(1)} copy-done((f32[56,9,128]{2,0,1:T(8,128)S(1)}, f32[56,9,128]{2,0,1:T(8,128)}, u32[]{:S(2)}) %copy-start) | copy-done | bytes 258072
  1.7 0.0 copy-start.1
  1.7 0.9 %copy-done.1 = f32[64,3,9,9]{0,1,3,2:T(4,128)S(1)} copy-done((f32[64,3,9,9]{0,1,3,2:T(4,128)S(1)}, f32[64,3,9,9]{0,1,3,2:T(4,128)}, u32[]{:S(2)}) %copy-start.1) | copy-done | bytes 62232
  2.6 0.0 copy-start.2
  2.6 0.9 %copy-done.2 = f32[64,4,9,9]{0,1,3,2:T(4,128)S(1)} copy-done((f32[64,4,9,9]{0,1,3,2:T(4,128)S(1)}, f32[64,4,9,9]{0,1,3,2:T(4,128)}, u32[]{:S(2)}) %copy-start.2) | copy-done | bytes 82968
  3.5 0.9 %copy-done.3 = f32[64,4,9,9]{0,1,3,2:T(4,128)S(1)} copy-done((f32[64,4,9,9]{0,1,3,2:T(4,128)S(1)}, f32[64,4,9,9]{0,1,3,2:T(4,128)}, u32[]{:S(2)}) %copy-start.3) | copy-done | bytes 82968
  4.4 0.9 %copy-done.4 = f32[3,56,56]{2,1,0:T(8,128)S(1)} copy-done((f32[3,56,56]{2,1,0:T(8,128)S(1)}, f32[3,56,56]{2,1,0:T(8,128)}, u32[]{:S(2)}) %copy-start.4) | copy-done | bytes 37656
  5.3 0.9 %copy-done.5 = f32[3,56,56]{2,1,0:T(8,128)S(1)} copy-done((f32[3,56,56]{2,1,0:T(8,128)S(1)}, f32[3,56,56]{2,1,0:T(8,128)}, u32[]{:S(2)}) %copy-start.5) | copy-done | bytes 37656
  6.2 0.8 %copy-done.6 = f32[4,21,56]{2,0,1:T(4,128)S(1)} copy-done((f32[4,21,56]{2,0,1:T(4,128)S(1)}, f32[4,21,56]{2,0,1:T(4,128)}, u32[]{:S(2)}) %copy-start.6) | copy-done | bytes 18840
  7.0 0.8 %copy-done.7 = f32[4,56,21]{1,0,2:T(4,128)S(1)} copy-done((f32[4,56,21]{1,0,2:T(4,128)S(1)}, f32[4,56,21]{1,0,2:T(4,128)}, u32[]{:S(2)}) %copy-start.7) | copy-done | bytes 18840
  7.8 0.8 %copy-done.8 = f32[3,21,21]{2,1,0:T(8,128)S(1)} copy-done((f32[3,21,21]{2,1,0:T(8,128)S(1)}, f32[3,21,21]{2,1,0:T(8,128)}, u32[]{:S(2)}) %copy-start.8) | copy-done | bytes 5316
  8.5 39.2 %elastic_step.1 = f32[9,56,128]{2,1,0:T(8,128)S(1)} custom-call(f32[9,56,128]{2,1,0:T(8,128)S(1)} %bitcast.17, s32[1,128]{1,0:T(1,128)S(1)} %bitcast.24, s32[1,128]{1,0:T(1,128)S(1)} %bitcast.25, s32[4,128]{1,0:T(4,128)S(1)} %copy-done.9, s32[4,128]{1,0:T(4,128)S(1)} %copy-done.10, s32[1,192]{1,0:T(1,128)S(1)} %bitcast.23, f32[3,56,56]{2,1,0:T(8,128)S(1)} %copy-done.4, ...), custom_call_target="tpu_custom_call" | custom-call | tf_op jit(solution)/shard_map/elastic_step/pallas_call | solution.py:327
  47.8 0.7 %copy.16 = f32[56,9,128]{2,0,1:T(8,128)} copy(f32[56,9,128]{2,0,1:T(8,128)S(1)} %bitcast.16) | data formatting | bytes 516096
  (6 shorter events, 0.0 us)
Async XLA Ops:
  0.0 0.7 %copy-start.13 = (s32[128]{0:T(128)S(1)}, s32[128]{0:T(128)}, u32[]{:S(2)}) copy-start(s32[128]{0:T(128)} %param.16) | copy-start | bytes 1540
  0.0 0.7 %copy-start.10 = (s32[4,128]{1,0:T(4,128)S(1)}, s32[4,128]{1,0:T(4,128)}, u32[]{:S(2)}) copy-start(s32[4,128]{1,0:T(4,128)} %flux.1) | copy-start | bytes 6148
  0.0 0.7 %copy-start.9 = (s32[4,128]{1,0:T(4,128)S(1)}, s32[4,128]{1,0:T(4,128)}, u32[]{:S(2)}) copy-start(s32[4,128]{1,0:T(4,128)} %neighbour.1) | copy-start | bytes 6148
  0.0 0.7 %copy-start.11 = (s32[192]{0:T(256)S(1)}, s32[192]{0:T(256)}, u32[]{:S(2)}) copy-start(s32[192]{0:T(256)} %param.19) | copy-start | bytes 2308
  0.0 0.7 %copy-start.12 = (s32[128]{0:T(128)S(1)}, s32[128]{0:T(128)}, u32[]{:S(2)}) copy-start(s32[128]{0:T(128)} %param.15) | copy-start | bytes 1540
  0.7 0.9 %copy-start = (f32[56,9,128]{2,0,1:T(8,128)S(1)}, f32[56,9,128]{2,0,1:T(8,128)}, u32[]{:S(2)}) copy-start(f32[56,9,128]{2,0,1:T(8,128)} %param.14) | copy-start | bytes 774148
  1.7 0.9 %copy-start.1 = (f32[64,3,9,9]{0,1,3,2:T(4,128)S(1)}, f32[64,3,9,9]{0,1,3,2:T(4,128)}, u32[]{:S(2)}) copy-start(f32[64,3,9,9]{0,1,3,2:T(4,128)} %param.25) | copy-start | bytes 186628
  2.6 0.9 %copy-start.2 = (f32[64,4,9,9]{0,1,3,2:T(4,128)S(1)}, f32[64,4,9,9]{0,1,3,2:T(4,128)}, u32[]{:S(2)}) copy-start(f32[64,4,9,9]{0,1,3,2:T(4,128)} %param.26) | copy-start | bytes 248836
  3.5 0.9 %copy-start.3 = (f32[64,4,9,9]{0,1,3,2:T(4,128)S(1)}, f32[64,4,9,9]{0,1,3,2:T(4,128)}, u32[]{:S(2)}) copy-start(f32[64,4,9,9]{0,1,3,2:T(4,128)} %param.27) | copy-start | bytes 248836
  4.4 0.9 %copy-start.4 = (f32[3,56,56]{2,1,0:T(8,128)S(1)}, f32[3,56,56]{2,1,0:T(8,128)}, u32[]{:S(2)}) copy-start(f32[3,56,56]{2,1,0:T(8,128)} %derivative.1) | copy-start | bytes 112900
  5.3 0.9 %copy-start.5 = (f32[3,56,56]{2,1,0:T(8,128)S(1)}, f32[3,56,56]{2,1,0:T(8,128)}, u32[]{:S(2)}) copy-start(f32[3,56,56]{2,1,0:T(8,128)} %stiffness.1) | copy-start | bytes 112900
  6.2 0.8 %copy-start.6 = (f32[4,21,56]{2,0,1:T(4,128)S(1)}, f32[4,21,56]{2,0,1:T(4,128)}, u32[]{:S(2)}) copy-start(f32[4,21,56]{2,0,1:T(4,128)} %param.22) | copy-start | bytes 56452
  7.0 0.8 %copy-start.7 = (f32[4,56,21]{1,0,2:T(4,128)S(1)}, f32[4,56,21]{1,0,2:T(4,128)}, u32[]{:S(2)}) copy-start(f32[4,56,21]{1,0,2:T(4,128)} %param.23) | copy-start | bytes 56452
  7.8 0.8 %copy-start.8 = (f32[3,21,21]{2,1,0:T(8,128)S(1)}, f32[3,21,21]{2,1,0:T(8,128)}, u32[]{:S(2)}) copy-start(f32[3,21,21]{2,1,0:T(8,128)} %orientation.1) | copy-start | bytes 15880
where the time goes:
time: 49 us; the launch traced here: 48.5 us
  Pallas kernels  39.2 us (80%)
  local copies, waits for them, and re-layouts  9.21 us (19%)
    pallas_call x1, Pallas kernels, body(): pl.pallas_call(functools.partial(kernel, n_dom, n_sub), name='elastic_ste...  39.2 us
    unnamed x29, local copies, waits for them, and re-layouts  9.21 us

commit v1 on v0

v1 whole, which is shorter than its diff:
```python
import functools
import math

import jax
import jax.numpy as jnp
from jax import lax
from jax.experimental import pallas as pl
from jax.experimental.pallas import tpu as pltpu
from jax.sharding import PartitionSpec as P

ORDER = 6
CAP_DOM = 64
CAP_SUB = 8
VARS = 9
BASIS = 56
FACE = 21
FPAD = 24
LANES = 128
CLASSES = 64
GHOSTS = 192
PAIRS = VARS * VARS
KDIM = 176
ROWS = VARS * FPAD
WIDE = 256
F32 = jnp.float32
BF16 = jnp.bfloat16
MESH = pl.DeviceIdType.MESH

half = 0.5
half_weights = [half ** (k + 1) / math.factorial(k + 1) for k in range(ORDER)]
late_weights = [(1.0 - half ** (k + 1)) / math.factorial(k + 1) for k in range(ORDER)]


def split(values):
    high = values.astype(BF16).astype(F32)
    return high, values - high


def left_operand(matrix, pad):
    high, low = split(matrix)
    parts = [high, low, high]
    if pad:
        parts.append(jnp.zeros((matrix.shape[0], pad), F32))
    return jnp.concatenate(parts, axis=1).astype(BF16)


def right_operand(values, pad):
    high, low = split(values)
    parts = [high, high, low]
    if pad:
        parts.append(jnp.zeros((pad, values.shape[1]), F32))
    return jnp.concatenate(parts, axis=0).astype(BF16)


def dot(left, right):
    return jnp.dot(left, right, preferred_element_type=F32)


def two_dots(values, right):
    high, low = split(values)
    return dot(high.astype(BF16), right) + dot(low.astype(BF16), right)


def kernel(
    n_dom,
    n_sub,
    remote,
    state_hbm,
    cluster_hbm,
    jacobian_hbm,
    neighbour_hbm,
    flux_hbm,
    send_hbm,
    derivative_hbm,
    stiffness_hbm,
    restriction_hbm,
    lifting_hbm,
    orientation_hbm,
    star_hbm,
    minus_hbm,
    plus_hbm,
    out,
    cluster,
    jacobian,
    neighbour,
    flux,
    send,
    derivative,
    stiffness,
    restriction,
    lifting,
    orientation,
    star,
    minus,
    plus,
    table,
    star_rows,
    minus_rows,
    plus_rows,
    left_derivative,
    left_stiffness,
    left_restriction,
    left_lifting,
    left_orientation,
    faces,
    turns,
    pick_send,
    pick_local,
    pick_ghost,
    current,
    moved,
    half_sum,
    late_sum,
    own,
    other,
    candidates,
    lift_in,
    payload,
    received,
    load_sem,
    send_sem,
    recv_sem,
):
    if remote:
        dom = lax.axis_index("dom")
        sub = lax.axis_index("sub")
        lower = lax.rem(dom + n_dom - 1, n_dom)
        upper = lax.rem(dom + 1, n_dom)
        peers = [(lower, sub), (upper, sub)]
        peers += [(dom, lax.rem(sub + i, n_sub)) for i in range(1, n_sub)]
        barrier = pltpu.get_barrier_semaphore()
        for peer in peers:
            pl.semaphore_signal(barrier, inc=1, device_id=peer, device_id_type=MESH)
    else:
        sub = 0

    loads = {}
    for i, (name, source, target) in enumerate(
        [
            ("jacobian", jacobian_hbm, jacobian),
            ("star", star_hbm, star),
            ("derivative", derivative_hbm, derivative),
            ("state", state_hbm, out),
            ("restriction", restriction_hbm, restriction),
            ("send", send_hbm, send),
            ("cluster", cluster_hbm, cluster),
            ("stiffness", stiffness_hbm, stiffness),
            ("flux", flux_hbm, flux),
            ("neighbour", neighbour_hbm, neighbour),
            ("minus", minus_hbm, minus),
            ("plus", plus_hbm, plus),
            ("orientation", orientation_hbm, orientation),
            ("lifting", lifting_hbm, lifting),
        ]
    ):
        loads[name] = pltpu.make_async_copy(source, target, load_sem.at[i])
        loads[name].start()

    def classes():
        class_id = lax.broadcasted_iota(jnp.int32, (CLASSES, LANES), 0)
        return (class_id == jacobian[...]).astype(F32).astype(BF16)

    loads["jacobian"].wait()
    loads["star"].wait()
    onehot = classes()
    for d in range(3):
        table[pl.ds(0, PAIRS), :] = two_dots(star[:, d, :], onehot)
        for p in range(VARS):
            star_rows[p, pl.ds(d * VARS, VARS), :] = table[pl.ds(p, VARS, stride=VARS), :]
    loads["derivative"].wait()
    for d in range(3):
        left_derivative[pl.ds(d * BASIS, BASIS), :] = left_operand(-derivative[d], 8)
    loads["restriction"].wait()
    faces[...] = jnp.zeros_like(faces)
    for f in range(4):
        faces[pl.ds(f * FPAD, FACE), :] = restriction[:, f, :]
    left_restriction[...] = left_operand(faces[...], 8)
    loads["send"].wait()
    send_column = jnp.transpose(jnp.broadcast_to(send[...], (8, GHOSTS)))[:, :1]
    lane = lax.broadcasted_iota(jnp.int32, (GHOSTS, 4 * LANES), 1)
    pick_send[...] = (lane == send_column).astype(F32).astype(BF16)
    candidates[...] = jnp.zeros_like(candidates)
    loads["cluster"].wait()
    loads["state"].wait()

    def rest_of_setup():
        loads["stiffness"].wait()
        for d in range(3):
            left_stiffness[pl.ds(d * BASIS, BASIS), :] = left_operand(stiffness[d], 8)
        loads["flux"].wait()
        loads["neighbour"].wait()

        def same(rows, target):
            index = lax.broadcasted_iota(jnp.int32, (rows, LANES), 0)
            return (index == target).astype(F32).astype(BF16)

        for f in range(4):
            code = neighbour[pl.ds(f, 1), :]
            face = flux[pl.ds(f, 1), :] // 3
            inner = jnp.where(code < LANES, face * LANES + code, -1)
            outer = code - LANES
            pick_local[:, pl.ds(f * LANES, LANES)] = same(4 * LANES, inner)
            pick_ghost[:, pl.ds(f * LANES, LANES)] = same(GHOSTS, outer)
        loads["minus"].wait()
        loads["plus"].wait()
        onehot = classes()
        for source, rows in ((minus, minus_rows), (plus, plus_rows)):
            table[...] = two_dots(source[...].reshape(4 * PAIRS, CLASSES), onehot)
            for p in range(VARS):
                for f in range(4):
                    rows[p, pl.ds(f * VARS, VARS), :] = table[
                        pl.ds(4 * p + f, VARS, stride=4 * VARS), :
                    ]
        loads["orientation"].wait()
        turns[...] = jnp.zeros_like(turns)
        for h in range(3):
            turns[pl.ds(h * FPAD, FACE), pl.ds(0, FACE)] = orientation[h]
        left_orientation[...] = left_operand(turns[...], 0)
        loads["lifting"].wait()
        for f in range(4):
            faces[pl.ds(f * FPAD, FACE), :] = lifting[:, f, :]
        left_lifting[...] = left_operand(jnp.transpose(faces[...]), 0)

    def mix(left, emit):
        right = jnp.concatenate([current[q] for q in range(VARS)], axis=1)
        result = dot(left[...], right)
        for d in range(3):
            for q in range(VARS):
                moved[d * VARS + q] = result[
                    d * BASIS : (d + 1) * BASIS, q * LANES : (q + 1) * LANES
                ]

        def one_variable(p, carry):
            total = None
            for k in range(3 * VARS):
                term = moved[k] * star_rows[p, pl.ds(k, 1), :]
                total = term if total is None else total + term
            emit(p, total)
            return carry

        lax.fori_loop(0, VARS, one_variable, 0)

    def weight(weights, degree):
        value = jnp.float32(weights[ORDER - 1])
        for k in range(ORDER - 2, 0, -1):
            value = jnp.where(degree == k, jnp.float32(weights[k]), value)
        return value

    def phase(step, carry):
        for q in range(VARS):
            values = out[q]
            current[q] = right_operand(values, 8)
            half_sum[q] = values * half_weights[0]
            late_sum[step, q] = values * late_weights[0]

        def degree_step(degree, carry):
            for_half = weight(half_weights, degree)
            for_late = weight(late_weights, degree)

            def emit(p, values):
                half_sum[p] += values * for_half
                late_sum[step, p] += values * for_late
                current[p] = right_operand(values, 8)

            mix(left_derivative, emit)
            return carry

        lax.fori_loop(1, ORDER, degree_step, 0)

        use_half = jnp.logical_or(cluster[...] == 1, step == 0)
        for q in range(VARS):
            current[q] = right_operand(jnp.where(use_half, half_sum[q], late_sum[0, q]), 8)

        right = jnp.concatenate([current[q] for q in range(VARS)], axis=1)
        projected = dot(left_restriction[...], right)
        for q in range(VARS):
            for f in range(4):
                tile = projected[f * FPAD : (f + 1) * FPAD, q * LANES : (q + 1) * LANES]
                own[f * VARS + q] = tile
                high, low = split(tile)
                lanes = pl.ds(f * LANES, LANES)
                candidates[pl.ds(q * FPAD, FPAD), lanes] = high.astype(BF16)
                candidates[pl.ds(WIDE + q * FPAD, FPAD), lanes] = low.astype(BF16)

        both = lax.dot_general(
            pick_send[...], candidates[...], (((1,), (1,)), ((), ())), preferred_element_type=F32
        )
        payload[step] = both[:, :WIDE] + both[:, WIDE:]
        copies = []
        if remote:

            @pl.when(step == 0)
            def _():
                pl.semaphore_wait(barrier, len(peers))

            for i, peer in enumerate(peers):
                if i == 0:
                    source, target, count = 0, CAP_DOM, CAP_DOM
                elif i == 1:
                    source, target, count = CAP_DOM, 0, CAP_DOM
                else:
                    source = pl.multiple_of(2 * CAP_DOM + peer[1] * CAP_SUB, CAP_SUB)
                    target = pl.multiple_of(2 * CAP_DOM + sub * CAP_SUB, CAP_SUB)
                    count = CAP_SUB
                copy = pltpu.make_async_remote_copy(
                    src_ref=payload.at[step, pl.ds(source, count), :],
                    dst_ref=received.at[step, pl.ds(target, count), :],
                    send_sem=send_sem.at[step, i],
                    recv_sem=recv_sem.at[step, i],
                    device_id=peer,
                    device_id_type=MESH,
                )
                copy.start()
                copies.append(copy)
        mine = pl.multiple_of(2 * CAP_DOM + sub * CAP_SUB, CAP_SUB)
        received[step, pl.ds(mine, CAP_SUB), :] = payload[step, pl.ds(mine, CAP_SUB), :]

        @pl.when(step == 0)
        def _():
            rest_of_setup()

        def add_volume(p, values):
            out[p] += values

        mix(left_stiffness, add_volume)

        turn = lax.rem(flux[...], 3)

        def orient(values):
            for q in range(VARS):
                turned = dot(
                    left_orientation[...], right_operand(values[q * FPAD : (q + 1) * FPAD], 0)
                )
                for f in range(4):
                    lanes = slice(f * LANES, (f + 1) * LANES)
                    which = turn[f : f + 1]
                    other[f * VARS + q] = jnp.where(
                        which == 0,
                        turned[:FPAD, lanes],
                        jnp.where(
                            which == 1,
                            turned[FPAD : 2 * FPAD, lanes],
                            turned[2 * FPAD :, lanes],
                        ),
                    )

        def lift():
            right = jnp.concatenate([lift_in[p] for p in range(VARS)], axis=1)
            lifted = dot(left_lifting[...], right)
            for p in range(VARS):
                out[p] += lifted[:, p * LANES : (p + 1) * LANES]

        orient(
            dot(candidates[pl.ds(0, ROWS), :], pick_local[...])
            + dot(candidates[pl.ds(WIDE, ROWS), :], pick_local[...])
        )

        def both_sides(p, carry):
            tiles = []
            for f in range(4):
                total = None
                for q in range(VARS):
                    k = f * VARS + q
                    term = (
                        own[k] * minus_rows[p, pl.ds(k, 1), :]
                        + other[k] * plus_rows[p, pl.ds(k, 1), :]
                    )
                    total = term if total is None else total + term
                tiles.append(total)
            lift_in[p] = right_operand(jnp.concatenate(tiles, axis=0), 0)
            return carry

        lax.fori_loop(0, VARS, both_sides, 0)
        lift()

        for copy in copies:
            copy.wait()
        ghosts = jnp.transpose(received[step])[:ROWS]
        orient(two_dots(ghosts, pick_ghost[...]))

        def other_side(p, carry):
            tiles = []
            for f in range(4):
                total = None
                for q in range(VARS):
                    k = f * VARS + q
                    term = other[k] * plus_rows[p, pl.ds(k, 1), :]
                    total = term if total is None else total + term
                tiles.append(total)
            lift_in[p] = right_operand(jnp.concatenate(tiles, axis=0), 0)
            return carry

        lax.fori_loop(0, VARS, other_side, 0)
        lift()
        return carry

    lax.fori_loop(0, 2, phase, 0)


def body(
    modal_state,
    cluster_id,
    jacobian_id,
    face_neighbour,
    flux_index,
    send_list,
    derivative,
    stiffness,
    restriction,
    lifting,
    orientation,
    star_matrix,
    flux_minus,
    flux_plus,
    remote=True,
):
    n_dom, n_sub = (lax.axis_size("dom"), lax.axis_size("sub")) if remote else (1, 1)
    operands = (
        jnp.transpose(modal_state, (1, 0, 2)),
        cluster_id.reshape(1, LANES),
        jacobian_id.reshape(1, LANES),
        face_neighbour,
        flux_index,
        send_list.reshape(1, GHOSTS),
        derivative,
        stiffness,
        jnp.transpose(restriction, (1, 0, 2)),
        jnp.transpose(lifting, (2, 0, 1)),
        orientation,
        jnp.transpose(star_matrix, (2, 3, 1, 0)).reshape(PAIRS, 3, CLASSES),
        jnp.transpose(flux_minus, (2, 3, 1, 0)).reshape(PAIRS, 4, CLASSES),
        jnp.transpose(flux_plus, (2, 3, 1, 0)).reshape(PAIRS, 4, CLASSES),
    )
    n_peers = n_sub + 1
    result = pl.pallas_call(
        functools.partial(kernel, n_dom, n_sub, remote),
        name="elastic_step",
        out_shape=jax.ShapeDtypeStruct((VARS, BASIS, LANES), F32),
        in_specs=[pl.BlockSpec(memory_space=pl.ANY)] * len(operands),
        out_specs=pl.BlockSpec(memory_space=pltpu.VMEM),
        scratch_shapes=[pltpu.VMEM(x.shape, x.dtype) for x in operands[1:]]
        + [
            pltpu.VMEM((4 * PAIRS, LANES), F32),
            pltpu.VMEM((VARS, 32, LANES), F32),
            pltpu.VMEM((VARS, 40, LANES), F32),
            pltpu.VMEM((VARS, 40, LANES), F32),
            pltpu.VMEM((3 * BASIS, KDIM), BF16),
            pltpu.VMEM((3 * BASIS, KDIM), BF16),
            pltpu.VMEM((4 * FPAD, KDIM), BF16),
            pltpu.VMEM((BASIS, 12 * FPAD), BF16),
            pltpu.VMEM((3 * FPAD, 3 * FPAD), BF16),
            pltpu.VMEM((4 * FPAD, BASIS), F32),
            pltpu.VMEM((3 * FPAD, FPAD), F32),
            pltpu.VMEM((GHOSTS, 4 * LANES), BF16),
            pltpu.VMEM((4 * LANES, 4 * LANES), BF16),
            pltpu.VMEM((GHOSTS, 4 * LANES), BF16),
            pltpu.VMEM((VARS, KDIM, LANES), BF16),
            pltpu.VMEM((3 * VARS, BASIS, LANES), F32),
            pltpu.VMEM((VARS, BASIS, LANES), F32),
            pltpu.VMEM((2, VARS, BASIS, LANES), F32),
            pltpu.VMEM((4 * VARS, FPAD, LANES), F32),
            pltpu.VMEM((4 * VARS, FPAD, LANES), F32),
            pltpu.VMEM((2 * WIDE, 4 * LANES), BF16),
            pltpu.VMEM((VARS, 12 * FPAD, LANES), BF16),
            pltpu.VMEM((2, GHOSTS, WIDE), F32),
            pltpu.VMEM((2, GHOSTS, WIDE), F32),
            pltpu.SemaphoreType.DMA((len(operands),)),
            pltpu.SemaphoreType.DMA((2, n_peers)),
            pltpu.SemaphoreType.DMA((2, n_peers)),
        ],
        compiler_params=pltpu.CompilerParams(
            collective_id=0 if remote else None,
            has_side_effects=True,
            vmem_limit_bytes=60 * 1024 * 1024,
        ),
    )(*operands)
    return jnp.transpose(result, (1, 0, 2))


def solution(mesh):
    placed = (
        P(None, None, ("dom", "sub")),
        P(("dom", "sub")),
        P(("dom", "sub")),
        P(None, ("dom", "sub")),
        P(None, ("dom", "sub")),
        P(("dom", "sub")),
        P(),
        P(),
        P(),
        P(),
        P(),
        P(),
        P(),
        P(),
    )
    return jax.shard_map(
        body, mesh=mesh, in_specs=placed, out_specs=P(None, None, ("dom", "sub")), check_vma=False
    )
```

time: 49 us -> 43.3 us (0.88)
  local copies, waits for them, and re-layouts: 9.21 us -> 1.66 us
  Pallas kernels: 39.2 us -> 41.5 us
    unnamed x29 -> x1, local copies, waits for them, and re-layouts: 9.21 us -> 1.66 us
    pallas_call x1, Pallas kernels: 39.2 us -> 41.5 us  [body(): pl.pallas_call(functools.partial(kernel, n_dom, n_sub, remote), name='ela...]
where the time goes in v1:
time: 43.3 us; the launch traced here: 43.1 us
  Pallas kernels  41.5 us (96%)
  local copies, waits for them, and re-layouts  1.66 us (4%)
    pallas_call x1, Pallas kernels, body(): pl.pallas_call(functools.partial(kernel, n_dom, n_sub, remote), name='ela...  41.5 us
    unnamed x1, local copies, waits for them, and re-layouts  1.66 us

profile of v1, /device:TPU:1, one launch (start us, length us, event | category | flops | bytes accessed | tf_op | source)
XLA Modules:
  0.0 43.1 jit_solution(12868718707043889318)
XLA Ops:
  0.0 41.5 %elastic_step.1 = f32[9,56,128]{2,1,0:T(8,128)} custom-call(f32[9,56,128]{2,1,0:T(8,128)} %bitcast.17, s32[1,128]{1,0:T(1,128)} %bitcast.24, s32[1,128]{1,0:T(1,128)} %bitcast.25, s32[4,128]{1,0:T(4,128)} %neighbour_hbm.1, s32[4,128]{1,0:T(4,128)} %flux_hbm.1, s32[1,192]{1,0:T(1,128)} %bitcast.23, f32[3,56,56]{2,1,0:T(8,128)} %derivative_hbm.1, ...), custom_call_target="tpu_custom_call" | custom-call | tf_op jit(solution)/shard_map/elastic_step/pallas_call | solution.py:435
  41.5 1.7 %copy.16 = f32[56,9,128]{2,0,1:T(8,128)} copy(f32[56,9,128]{2,0,1:T(8,128)} %bitcast.16) | data formatting | bytes 516096

commit v2 on v1

--- a/solution.py
+++ b/solution.py
@@ -22,6 +22,7 @@
 KDIM = 176
 ROWS = VARS * FPAD
 WIDE = 256
+SLOTS = 256
 F32 = jnp.float32
 BF16 = jnp.bfloat16
 MESH = pl.DeviceIdType.MESH
@@ -109,18 +110,24 @@
     pick_ghost,
     current,
     moved,
+    moved_next,
     half_sum,
     late_sum,
     own,
     other,
     candidates,
     lift_in,
+    mixed,
+    slot_table,
+    slot_rows,
+    slot_turn,
     payload,
     received,
     load_sem,
     send_sem,
     recv_sem,
 ):
+    received[:, pl.ds(GHOSTS, SLOTS - GHOSTS), :] = jnp.zeros((2, SLOTS - GHOSTS, WIDE), F32)
     if remote:
         dom = lax.axis_index("dom")
         sub = lax.axis_index("sub")
@@ -138,7 +145,7 @@
     for i, (name, source, target) in enumerate(
         [
             ("jacobian", jacobian_hbm, jacobian),
-            ("star", star_hbm, star),
+            ("star", star_hbm, star.at[:, pl.ds(0, 3), :]),
             ("derivative", derivative_hbm, derivative),
             ("state", state_hbm, out),
             ("restriction", restriction_hbm, restriction),
@@ -163,10 +170,12 @@
     loads["jacobian"].wait()
     loads["star"].wait()
     onehot = classes()
+    table[...] = two_dots(star[...].reshape(4 * PAIRS, CLASSES), onehot)
     for d in range(3):
-        table[pl.ds(0, PAIRS), :] = two_dots(star[:, d, :], onehot)
         for p in range(VARS):
-            star_rows[p, pl.ds(d * VARS, VARS), :] = table[pl.ds(p, VARS, stride=VARS), :]
+            star_rows[p, pl.ds(d * VARS, VARS), :] = table[
+                pl.ds(4 * p + d, VARS, stride=4 * VARS), :
+            ]
     loads["derivative"].wait()
     for d in range(3):
         left_derivative[pl.ds(d * BASIS, BASIS), :] = left_operand(-derivative[d], 8)
@@ -178,7 +187,8 @@
     loads["send"].wait()
     send_column = jnp.transpose(jnp.broadcast_to(send[...], (8, GHOSTS)))[:, :1]
     lane = lax.broadcasted_iota(jnp.int32, (GHOSTS, 4 * LANES), 1)
-    pick_send[...] = (lane == send_column).astype(F32).astype(BF16)
+    pick_send[pl.ds(0, GHOSTS), :] = (lane == send_column).astype(F32).astype(BF16)
+    pick_send[pl.ds(GHOSTS, SLOTS - GHOSTS), :] = jnp.zeros((SLOTS - GHOSTS, 4 * LANES), BF16)
     candidates[...] = jnp.zeros_like(candidates)
     loads["cluster"].wait()
     loads["state"].wait()
@@ -200,7 +210,7 @@
             inner = jnp.where(code < LANES, face * LANES + code, -1)
             outer = code - LANES
             pick_local[:, pl.ds(f * LANES, LANES)] = same(4 * LANES, inner)
-            pick_ghost[:, pl.ds(f * LANES, LANES)] = same(GHOSTS, outer)
+            pick_ghost[:, pl.ds(f * LANES, LANES)] = same(SLOTS, outer)
         loads["minus"].wait()
         loads["plus"].wait()
         onehot = classes()
@@ -211,6 +221,39 @@
                     rows[p, pl.ds(f * VARS, VARS), :] = table[
                         pl.ds(4 * p + f, VARS, stride=4 * VARS), :
                     ]
+            if rows is plus_rows:
+                attributes = jnp.concatenate(
+                    [
+                        jnp.concatenate([jacobian[...]] * 4, axis=1),
+                        jnp.concatenate([lax.rem(flux[pl.ds(f, 1), :], 3) for f in range(4)], axis=1),
+                        jnp.concatenate([jnp.full((1, LANES), f, jnp.int32) for f in range(4)], axis=1),
+                        jnp.zeros((5, 4 * LANES), jnp.int32),
+                    ],
+                    axis=0,
+                )
+                slot_data = lax.dot_general(
+                    attributes.astype(F32).astype(BF16),
+                    pick_send[...],
+                    (((1,), (1,)), ((), ())),
+                    preferred_element_type=F32,
+                ).astype(jnp.int32)
+                slot_turn[...] = slot_data[1:2]
+                slot_face = slot_data[2:3]
+                slot_class = lax.broadcasted_iota(jnp.int32, (CLASSES, SLOTS), 0) == slot_data[:1]
+                looked_up = two_dots(
+                    source[...].reshape(4 * PAIRS, CLASSES), slot_class.astype(F32).astype(BF16)
+                )
+                for half_of in range(SLOTS // LANES):
+                    slot_table[half_of] = looked_up[:, half_of * LANES : (half_of + 1) * LANES]
+                for p in range(VARS):
+                    for half_of in range(SLOTS // LANES):
+                        lanes = slice(half_of * LANES, (half_of + 1) * LANES)
+                        face = slot_face[:, lanes]
+                        chosen = None
+                        for f in range(4):
+                            mine = slot_table[half_of, pl.ds(4 * p + f, VARS, stride=4 * VARS), :]
+                            chosen = mine if f == 0 else jnp.where(face == f, mine, chosen)
+                        slot_rows[p, pl.ds(0, VARS), lanes] = chosen
         loads["orientation"].wait()
         turns[...] = jnp.zeros_like(turns)
         for h in range(3):
@@ -221,24 +264,35 @@
             faces[pl.ds(f * FPAD, FACE), :] = lifting[:, f, :]
         left_lifting[...] = left_operand(jnp.transpose(faces[...]), 0)
 
-    def mix(left, emit):
-        right = jnp.concatenate([current[q] for q in range(VARS)], axis=1)
+    def project(left, group, target):
+        right = current[group[0]]
+        if len(group) > 1:
+            right = jnp.concatenate([current[q] for q in group], axis=1)
         result = dot(left[...], right)
         for d in range(3):
-            for q in range(VARS):
-                moved[d * VARS + q] = result[
-                    d * BASIS : (d + 1) * BASIS, q * LANES : (q + 1) * LANES
+            for i, q in enumerate(group):
+                target[d * VARS + q] = result[
+                    d * BASIS : (d + 1) * BASIS, i * LANES : (i + 1) * LANES
                 ]
 
+    def mix_several(first_var, count, source):
+        totals = [None] * count
+        for k in range(3 * VARS):
+            block = source[k]
+            for i in range(count):
+                term = block * star_rows[first_var + i, pl.ds(k, 1), :]
+                totals[i] = term if totals[i] is None else totals[i] + term
+        return totals
+
+    def mix(left, emit):
+        project(left, range(VARS), moved)
+
         def one_variable(p, carry):
-            total = None
-            for k in range(3 * VARS):
-                term = moved[k] * star_rows[p, pl.ds(k, 1), :]
-                total = term if total is None else total + term
-            emit(p, total)
+            for i, values in enumerate(mix_several(3 * p, 3, moved)):
+                emit(3 * p + i, values)
             return carry
 
-        lax.fori_loop(0, VARS, one_variable, 0)
+        lax.fori_loop(0, VARS // 3, one_variable, 0)
 
     def weight(weights, degree):
         value = jnp.float32(weights[ORDER - 1])
@@ -253,19 +307,31 @@
             half_sum[q] = values * half_weights[0]
             late_sum[step, q] = values * late_weights[0]
 
-        def degree_step(degree, carry):
+        def degree_step(degree, source, target):
             for_half = weight(half_weights, degree)
             for_late = weight(late_weights, degree)
 
-            def emit(p, values):
-                half_sum[p] += values * for_half
-                late_sum[step, p] += values * for_late
-                current[p] = right_operand(values, 8)
-
-            mix(left_derivative, emit)
+            def some_variables(first_var, count):
+                for i, values in enumerate(mix_several(first_var, count, source)):
+                    p = first_var + i
+                    half_sum[p] += values * for_half
+                    late_sum[step, p] += values * for_late
+                    current[p] = right_operand(values, 8)
+
+            for first_var in range(0, VARS, 3):
+                some_variables(first_var, 3)
+                if target is not None:
+                    project(left_derivative, range(first_var, first_var + 3), target)
+
+        project(left_derivative, range(VARS), moved)
+
+        def two_degrees(i, carry):
+            degree_step(2 * i + 1, moved, moved_next)
+            degree_step(2 * i + 2, moved_next, moved)
             return carry
 
-        lax.fori_loop(1, ORDER, degree_step, 0)
+        lax.fori_loop(0, 2, two_degrees, 0)
+        degree_step(5, moved, None)
 
         use_half = jnp.logical_or(cluster[...] == 1, step == 0)
         for q in range(VARS):
@@ -283,7 +349,10 @@
                 candidates[pl.ds(WIDE + q * FPAD, FPAD), lanes] = low.astype(BF16)
 
         both = lax.dot_general(
-            pick_send[...], candidates[...], (((1,), (1,)), ((), ())), preferred_element_type=F32
+            pick_send[pl.ds(0, GHOSTS), :],
+            candidates[...],
+            (((1,), (1,)), ((), ())),
+            preferred_element_type=F32,
         )
         payload[step] = both[:, :WIDE] + both[:, WIDE:]
         copies = []
@@ -375,22 +444,36 @@
 
         for copy in copies:
             copy.wait()
-        ghosts = jnp.transpose(received[step])[:ROWS]
-        orient(two_dots(ghosts, pick_ghost[...]))
-
-        def other_side(p, carry):
-            tiles = []
-            for f in range(4):
-                total = None
-                for q in range(VARS):
-                    k = f * VARS + q
-                    term = other[k] * plus_rows[p, pl.ds(k, 1), :]
-                    total = term if total is None else total + term
-                tiles.append(total)
+        ghosts = jnp.transpose(received[step])
+        turned = dot(
+            left_orientation[...],
+            jnp.concatenate(
+                [right_operand(ghosts[q * FPAD : (q + 1) * FPAD], 0) for q in range(VARS)], axis=1
+            ),
+        )
+        which = slot_turn[...]
+        aligned = []
+        for q in range(VARS):
+            tile = turned[:, q * SLOTS : (q + 1) * SLOTS]
+            aligned.append(
+                jnp.where(
+                    which == 0,
+                    tile[:FPAD],
+                    jnp.where(which == 1, tile[FPAD : 2 * FPAD], tile[2 * FPAD :]),
+                )
+            )
+        for p in range(VARS):
+            total = None
+            for q in range(VARS):
+                term = aligned[q] * slot_rows[p, pl.ds(q, 1), :]
+                total = term if total is None else total + term
+            mixed[pl.ds(p * FPAD, FPAD), :] = total
+        scattered = two_dots(mixed[...], pick_ghost[...])
+        for p in range(VARS):
+            tiles = [
+                scattered[p * FPAD : (p + 1) * FPAD, f * LANES : (f + 1) * LANES] for f in range(4)
+            ]
             lift_in[p] = right_operand(jnp.concatenate(tiles, axis=0), 0)
-            return carry
-
-        lax.fori_loop(0, VARS, other_side, 0)
         lift()
         return carry
 
@@ -431,14 +514,18 @@
         jnp.transpose(flux_minus, (2, 3, 1, 0)).reshape(PAIRS, 4, CLASSES),
         jnp.transpose(flux_plus, (2, 3, 1, 0)).reshape(PAIRS, 4, CLASSES),
     )
+    operands = tuple(pltpu.with_memory_space_constraint(x, pltpu.HBM) for x in operands)
     n_peers = n_sub + 1
     result = pl.pallas_call(
         functools.partial(kernel, n_dom, n_sub, remote),
         name="elastic_step",
         out_shape=jax.ShapeDtypeStruct((VARS, BASIS, LANES), F32),
-        in_specs=[pl.BlockSpec(memory_space=pl.ANY)] * len(operands),
+        in_specs=[pl.BlockSpec(memory_space=pltpu.HBM)] * len(operands),
         out_specs=pl.BlockSpec(memory_space=pltpu.VMEM),
-        scratch_shapes=[pltpu.VMEM(x.shape, x.dtype) for x in operands[1:]]
+        scratch_shapes=[
+            pltpu.VMEM((PAIRS, 4, CLASSES) if x is operands[11] else x.shape, x.dtype)
+            for x in operands[1:]
+        ]
         + [
             pltpu.VMEM((4 * PAIRS, LANES), F32),
             pltpu.VMEM((VARS, 32, LANES), F32),
@@ -451,10 +538,11 @@
             pltpu.VMEM((3 * FPAD, 3 * FPAD), BF16),
             pltpu.VMEM((4 * FPAD, BASIS), F32),
             pltpu.VMEM((3 * FPAD, FPAD), F32),
-            pltpu.VMEM((GHOSTS, 4 * LANES), BF16),
+            pltpu.VMEM((SLOTS, 4 * LANES), BF16),
             pltpu.VMEM((4 * LANES, 4 * LANES), BF16),
-            pltpu.VMEM((GHOSTS, 4 * LANES), BF16),
+            pltpu.VMEM((SLOTS, 4 * LANES), BF16),
             pltpu.VMEM((VARS, KDIM, LANES), BF16),
+            pltpu.VMEM((3 * VARS, BASIS, LANES), F32),
             pltpu.VMEM((3 * VARS, BASIS, LANES), F32),
             pltpu.VMEM((VARS, BASIS, LANES), F32),
             pltpu.VMEM((2, VARS, BASIS, LANES), F32),
@@ -462,8 +550,12 @@
             pltpu.VMEM((4 * VARS, FPAD, LANES), F32),
             pltpu.VMEM((2 * WIDE, 4 * LANES), BF16),
             pltpu.VMEM((VARS, 12 * FPAD, LANES), BF16),
+            pltpu.VMEM((ROWS, SLOTS), F32),
+            pltpu.VMEM((2, 4 * PAIRS, LANES), F32),
+            pltpu.VMEM((VARS, 16, SLOTS), F32),
+            pltpu.VMEM((1, SLOTS), jnp.int32),
             pltpu.VMEM((2, GHOSTS, WIDE), F32),
-            pltpu.VMEM((2, GHOSTS, WIDE), F32),
+            pltpu.VMEM((2, SLOTS, WIDE), F32),
             pltpu.SemaphoreType.DMA((len(operands),)),
             pltpu.SemaphoreType.DMA((2, n_peers)),
             pltpu.SemaphoreType.DMA((2, n_peers)),
@@ -471,7 +563,7 @@
         compiler_params=pltpu.CompilerParams(
             collective_id=0 if remote else None,
             has_side_effects=True,
-            vmem_limit_bytes=60 * 1024 * 1024,
+            vmem_limit_bytes=24 * 1024 * 1024,
         ),
     )(*operands)
     return jnp.transpose(result, (1, 0, 2))

time: 43.3 us -> 38.8 us (0.90)
  Pallas kernels: 41.5 us -> 38 us
  local copies, waits for them, and re-layouts: 1.66 us -> 0.7 us
    pallas_call x1, Pallas kernels: 41.5 us -> 38 us  [body(): pl.pallas_call(functools.partial(kernel, n_dom, n_sub, remote), name='ela...]
    unnamed x1, local copies, waits for them, and re-layouts: 1.66 us -> 0.7 us
where the time goes in v2:
time: 38.8 us; the launch traced here: 38.7 us
  Pallas kernels  38 us (98%)
  local copies, waits for them, and re-layouts  0.7 us (2%)
    pallas_call x1, Pallas kernels, body(): pl.pallas_call(functools.partial(kernel, n_dom, n_sub, remote), name='ela...  38 us

profile of v2, /device:TPU:1, one launch (start us, length us, event | category | flops | bytes accessed | tf_op | source)
XLA Modules:
  0.0 38.7 jit_solution(5524220822472671780)
XLA Ops:
  0.0 38.0 %elastic_step.1 = f32[9,56,128]{2,1,0:T(8,128)S(1)} custom-call(f32[9,56,128]{2,1,0:T(8,128)} %bitcast.17, s32[1,128]{1,0:T(1,128)} %bitcast.24, s32[1,128]{1,0:T(1,128)} %bitcast.25, s32[4,128]{1,0:T(4,128)} %neighbour_hbm.1, s32[4,128]{1,0:T(4,128)} %flux_hbm.1, s32[1,192]{1,0:T(1,128)} %bitcast.23, f32[3,56,56]{2,1,0:T(8,128)} %derivative_hbm.1, ...), custom_call_target="tpu_custom_call" | custom-call | tf_op jit(solution)/shard_map/elastic_step/pallas_call | solution.py:519
  38.0 0.7 %copy.16 = f32[56,9,128]{2,0,1:T(8,128)} copy(f32[56,9,128]{2,0,1:T(8,128)S(1)} %bitcast.16) | data formatting | bytes 516096

commit v3 on v2

--- a/solution.py
+++ b/solution.py
@@ -113,6 +113,7 @@
     moved_next,
     half_sum,
     late_sum,
+    terms,
     own,
     other,
     candidates,
@@ -127,17 +128,23 @@
     send_sem,
     recv_sem,
 ):
-    received[:, pl.ds(GHOSTS, SLOTS - GHOSTS), :] = jnp.zeros((2, SLOTS - GHOSTS, WIDE), F32)
+    received[...] = jnp.zeros_like(received)
     if remote:
         dom = lax.axis_index("dom")
         sub = lax.axis_index("sub")
-        lower = lax.rem(dom + n_dom - 1, n_dom)
-        upper = lax.rem(dom + 1, n_dom)
-        peers = [(lower, sub), (upper, sub)]
-        peers += [(dom, lax.rem(sub + i, n_sub)) for i in range(1, n_sub)]
+        has_lower, has_upper = dom > 0, dom < n_dom - 1
+        lower = (jnp.maximum(dom - 1, 0), sub)
+        upper = (jnp.minimum(dom + 1, n_dom - 1), sub)
+        others = [(dom, lax.rem(sub + i, n_sub)) for i in range(1, n_sub)]
         barrier = pltpu.get_barrier_semaphore()
-        for peer in peers:
+
+        def greet(peer):
             pl.semaphore_signal(barrier, inc=1, device_id=peer, device_id_type=MESH)
+
+        for peer in others:
+            greet(peer)
+        pl.when(has_lower)(lambda: greet(lower))
+        pl.when(has_upper)(lambda: greet(upper))
     else:
         sub = 0
 
@@ -194,6 +201,11 @@
     loads["state"].wait()
 
     def rest_of_setup():
+        for q in range(VARS):
+            total = terms[0, q] * late_weights[0]
+            for k in range(1, ORDER):
+                total = total + terms[k, q] * late_weights[k]
+            late_sum[q] = total
         loads["stiffness"].wait()
         for d in range(3):
             left_stiffness[pl.ds(d * BASIS, BASIS), :] = left_operand(stiffness[d], 8)
@@ -305,17 +317,16 @@
             values = out[q]
             current[q] = right_operand(values, 8)
             half_sum[q] = values * half_weights[0]
-            late_sum[step, q] = values * late_weights[0]
+            terms[0, q] = values
 
         def degree_step(degree, source, target):
             for_half = weight(half_weights, degree)
-            for_late = weight(late_weights, degree)
 
             def some_variables(first_var, count):
                 for i, values in enumerate(mix_several(first_var, count, source)):
                     p = first_var + i
                     half_sum[p] += values * for_half
-                    late_sum[step, p] += values * for_late
+                    terms[degree, p] = values
                     current[p] = right_operand(values, 8)
 
             for first_var in range(0, VARS, 3):
@@ -335,7 +346,7 @@
 
         use_half = jnp.logical_or(cluster[...] == 1, step == 0)
         for q in range(VARS):
-            current[q] = right_operand(jnp.where(use_half, half_sum[q], late_sum[0, q]), 8)
+            current[q] = right_operand(jnp.where(use_half, half_sum[q], late_sum[q]), 8)
 
         right = jnp.concatenate([current[q] for q in range(VARS)], axis=1)
         projected = dot(left_restriction[...], right)
@@ -355,23 +366,16 @@
             preferred_element_type=F32,
         )
         payload[step] = both[:, :WIDE] + both[:, WIDE:]
-        copies = []
         if remote:
 
             @pl.when(step == 0)
             def _():
-                pl.semaphore_wait(barrier, len(peers))
-
-            for i, peer in enumerate(peers):
-                if i == 0:
-                    source, target, count = 0, CAP_DOM, CAP_DOM
-                elif i == 1:
-                    source, target, count = CAP_DOM, 0, CAP_DOM
-                else:
-                    source = pl.multiple_of(2 * CAP_DOM + peer[1] * CAP_SUB, CAP_SUB)
-                    target = pl.multiple_of(2 * CAP_DOM + sub * CAP_SUB, CAP_SUB)
-                    count = CAP_SUB
-                copy = pltpu.make_async_remote_copy(
+                pl.semaphore_wait(
+                    barrier, n_sub - 1 + has_lower.astype(jnp.int32) + has_upper.astype(jnp.int32)
+                )
+
+            def transfer(i, peer, source, target, count):
+                return pltpu.make_async_remote_copy(
                     src_ref=payload.at[step, pl.ds(source, count), :],
                     dst_ref=received.at[step, pl.ds(target, count), :],
                     send_sem=send_sem.at[step, i],
@@ -379,8 +383,22 @@
                     device_id=peer,
                     device_id_type=MESH,
                 )
+
+            def to_lower():
+                return transfer(0, lower, 0, CAP_DOM, CAP_DOM)
+
+            def to_upper():
+                return transfer(1, upper, CAP_DOM, 0, CAP_DOM)
+
+            target = pl.multiple_of(2 * CAP_DOM + sub * CAP_SUB, CAP_SUB)
+            copies = []
+            for i, peer in enumerate(others):
+                source = pl.multiple_of(2 * CAP_DOM + peer[1] * CAP_SUB, CAP_SUB)
+                copies.append(transfer(2 + i, peer, source, target, CAP_SUB))
+            pl.when(has_lower)(lambda: to_lower().start())
+            pl.when(has_upper)(lambda: to_upper().start())
+            for copy in copies:
                 copy.start()
-                copies.append(copy)
         mine = pl.multiple_of(2 * CAP_DOM + sub * CAP_SUB, CAP_SUB)
         received[step, pl.ds(mine, CAP_SUB), :] = payload[step, pl.ds(mine, CAP_SUB), :]
 
@@ -442,8 +460,20 @@
         lax.fori_loop(0, VARS, both_sides, 0)
         lift()
 
-        for copy in copies:
-            copy.wait()
+        if remote:
+            for copy in copies:
+                copy.wait()
+
+            @pl.when(has_lower)
+            def _():
+                to_lower().wait_send()
+                to_upper().wait_recv()
+
+            @pl.when(has_upper)
+            def _():
+                to_upper().wait_send()
+                to_lower().wait_recv()
+
         ghosts = jnp.transpose(received[step])
         turned = dot(
             left_orientation[...],
@@ -545,7 +575,8 @@
             pltpu.VMEM((3 * VARS, BASIS, LANES), F32),
             pltpu.VMEM((3 * VARS, BASIS, LANES), F32),
             pltpu.VMEM((VARS, BASIS, LANES), F32),
-            pltpu.VMEM((2, VARS, BASIS, LANES), F32),
+            pltpu.VMEM((VARS, BASIS, LANES), F32),
+            pltpu.VMEM((ORDER, VARS, BASIS, LANES), F32),
             pltpu.VMEM((4 * VARS, FPAD, LANES), F32),
             pltpu.VMEM((4 * VARS, FPAD, LANES), F32),
             pltpu.VMEM((2 * WIDE, 4 * LANES), BF16),

time: 38.8 us -> 32.1 us (0.83)
  Pallas kernels: 38 us -> 31.3 us
    pallas_call x1, Pallas kernels: 38 us -> 31.3 us  [body(): pl.pallas_call(functools.partial(kernel, n_dom, n_sub, remote), name='ela...]
where the time goes in v3:
time: 32.1 us; the launch traced here: 32 us
  Pallas kernels  31.3 us (98%)
  local copies, waits for them, and re-layouts  0.7 us (2%)
    pallas_call x1, Pallas kernels, body(): pl.pallas_call(functools.partial(kernel, n_dom, n_sub, remote), name='ela...  31.3 us
    unnamed x1, local copies, waits for them, and re-layouts  0.7 us

profile of v3, /device:TPU:1, one launch (start us, length us, event | category | flops | bytes accessed | tf_op | source)
XLA Modules:
  0.0 32.0 jit_solution(15255208827850379367)
XLA Ops:
  0.0 31.3 %elastic_step.1 = f32[9,56,128]{2,1,0:T(8,128)S(1)} custom-call(f32[9,56,128]{2,1,0:T(8,128)} %bitcast.17, s32[1,128]{1,0:T(1,128)} %bitcast.24, s32[1,128]{1,0:T(1,128)} %bitcast.25, s32[4,128]{1,0:T(4,128)} %neighbour_hbm.1, s32[4,128]{1,0:T(4,128)} %flux_hbm.1, s32[1,192]{1,0:T(1,128)} %bitcast.23, f32[3,56,56]{2,1,0:T(8,128)} %derivative_hbm.1, ...), custom_call_target="tpu_custom_call" | custom-call | tf_op jit(solution)/shard_map/elastic_step/pallas_call | solution.py:549
  31.3 0.7 %copy.16 = f32[56,9,128]{2,0,1:T(8,128)} copy(f32[56,9,128]{2,0,1:T(8,128)S(1)} %bitcast.16) | data formatting | bytes 516096

commit v4 on v3

--- a/solution.py
+++ b/solution.py
@@ -23,6 +23,7 @@
 ROWS = VARS * FPAD
 WIDE = 256
 SLOTS = 256
+lead, rest = range(0, 3), range(3, 9)
 F32 = jnp.float32
 BF16 = jnp.bfloat16
 MESH = pl.DeviceIdType.MESH
@@ -110,7 +111,7 @@
     pick_ghost,
     current,
     moved,
-    moved_next,
+    partial,
     half_sum,
     late_sum,
     terms,
@@ -128,26 +129,6 @@
     send_sem,
     recv_sem,
 ):
-    received[...] = jnp.zeros_like(received)
-    if remote:
-        dom = lax.axis_index("dom")
-        sub = lax.axis_index("sub")
-        has_lower, has_upper = dom > 0, dom < n_dom - 1
-        lower = (jnp.maximum(dom - 1, 0), sub)
-        upper = (jnp.minimum(dom + 1, n_dom - 1), sub)
-        others = [(dom, lax.rem(sub + i, n_sub)) for i in range(1, n_sub)]
-        barrier = pltpu.get_barrier_semaphore()
-
-        def greet(peer):
-            pl.semaphore_signal(barrier, inc=1, device_id=peer, device_id_type=MESH)
-
-        for peer in others:
-            greet(peer)
-        pl.when(has_lower)(lambda: greet(lower))
-        pl.when(has_upper)(lambda: greet(upper))
-    else:
-        sub = 0
-
     loads = {}
     for i, (name, source, target) in enumerate(
         [
@@ -170,10 +151,44 @@
         loads[name] = pltpu.make_async_copy(source, target, load_sem.at[i])
         loads[name].start()
 
+    received[...] = jnp.zeros_like(received)
+    candidates[...] = jnp.zeros_like(candidates)
+    faces[...] = jnp.zeros_like(faces)
+    if remote:
+        dom = lax.axis_index("dom")
+        sub = lax.axis_index("sub")
+        has_lower, has_upper = dom > 0, dom < n_dom - 1
+        lower = (jnp.maximum(dom - 1, 0), sub)
+        upper = (jnp.minimum(dom + 1, n_dom - 1), sub)
+        others = [(dom, lax.rem(sub + i, n_sub)) for i in range(1, n_sub)]
+        barrier = pltpu.get_barrier_semaphore()
+
+        def greet(peer):
+            pl.semaphore_signal(barrier, inc=1, device_id=peer, device_id_type=MESH)
+
+        for peer in others:
+            greet(peer)
+        pl.when(has_lower)(lambda: greet(lower))
+        pl.when(has_upper)(lambda: greet(upper))
+    else:
+        sub = 0
+
     def classes():
         class_id = lax.broadcasted_iota(jnp.int32, (CLASSES, LANES), 0)
         return (class_id == jacobian[...]).astype(F32).astype(BF16)
 
+    loads["derivative"].wait()
+    for d in range(3):
+        left_derivative[pl.ds(d * BASIS, BASIS), :] = left_operand(-derivative[d], 8)
+    loads["restriction"].wait()
+    for f in range(4):
+        faces[pl.ds(f * FPAD, FACE), :] = restriction[:, f, :]
+    left_restriction[...] = left_operand(faces[...], 8)
+    loads["send"].wait()
+    send_column = jnp.transpose(jnp.broadcast_to(send[...], (8, GHOSTS)))[:, :1]
+    lane = lax.broadcasted_iota(jnp.int32, (GHOSTS, 4 * LANES), 1)
+    pick_send[pl.ds(0, GHOSTS), :] = (lane == send_column).astype(F32).astype(BF16)
+    pick_send[pl.ds(GHOSTS, SLOTS - GHOSTS), :] = jnp.zeros((SLOTS - GHOSTS, 4 * LANES), BF16)
     loads["jacobian"].wait()
     loads["star"].wait()
     onehot = classes()
@@ -183,20 +198,6 @@
             star_rows[p, pl.ds(d * VARS, VARS), :] = table[
                 pl.ds(4 * p + d, VARS, stride=4 * VARS), :
             ]
-    loads["derivative"].wait()
-    for d in range(3):
-        left_derivative[pl.ds(d * BASIS, BASIS), :] = left_operand(-derivative[d], 8)
-    loads["restriction"].wait()
-    faces[...] = jnp.zeros_like(faces)
-    for f in range(4):
-        faces[pl.ds(f * FPAD, FACE), :] = restriction[:, f, :]
-    left_restriction[...] = left_operand(faces[...], 8)
-    loads["send"].wait()
-    send_column = jnp.transpose(jnp.broadcast_to(send[...], (8, GHOSTS)))[:, :1]
-    lane = lax.broadcasted_iota(jnp.int32, (GHOSTS, 4 * LANES), 1)
-    pick_send[pl.ds(0, GHOSTS), :] = (lane == send_column).astype(F32).astype(BF16)
-    pick_send[pl.ds(GHOSTS, SLOTS - GHOSTS), :] = jnp.zeros((SLOTS - GHOSTS, 4 * LANES), BF16)
-    candidates[...] = jnp.zeros_like(candidates)
     loads["cluster"].wait()
     loads["state"].wait()
 
@@ -307,6 +308,8 @@
         lax.fori_loop(0, VARS // 3, one_variable, 0)
 
     def weight(weights, degree):
+        if isinstance(degree, int):
+            return weights[degree]
         value = jnp.float32(weights[ORDER - 1])
         for k in range(ORDER - 2, 0, -1):
             value = jnp.where(degree == k, jnp.float32(weights[k]), value)
@@ -319,30 +322,58 @@
             half_sum[q] = values * half_weights[0]
             terms[0, q] = values
 
-        def degree_step(degree, source, target):
-            for_half = weight(half_weights, degree)
-
-            def some_variables(first_var, count):
-                for i, values in enumerate(mix_several(first_var, count, source)):
-                    p = first_var + i
-                    half_sum[p] += values * for_half
+        def accumulate(chosen, group, begin, degree=None):
+            totals = [None] * len(chosen)
+            for q in group:
+                for d in range(3):
+                    block = moved[d * VARS + q]
+                    for i, p in enumerate(chosen):
+                        term = block * star_rows[p, pl.ds(d * VARS + q, 1), :]
+                        totals[i] = term if totals[i] is None else totals[i] + term
+            for p, values in zip(chosen, totals):
+                if not begin:
+                    values = values + partial[p]
+                if degree is None:
+                    partial[p] = values
+                else:
+                    half_sum[p] += values * weight(half_weights, degree)
                     terms[degree, p] = values
                     current[p] = right_operand(values, 8)
 
-            for first_var in range(0, VARS, 3):
-                some_variables(first_var, 3)
-                if target is not None:
-                    project(left_derivative, range(first_var, first_var + 3), target)
-
-        project(left_derivative, range(VARS), moved)
-
-        def two_degrees(i, carry):
-            degree_step(2 * i + 1, moved, moved_next)
-            degree_step(2 * i + 2, moved_next, moved)
+        def first_part(degree):
+            project(left_derivative, rest, moved)
+            for chosen in [(0, 1, 2), (3, 4, 5), (6, 7, 8)]:
+                accumulate(chosen, lead, True)
+            for chosen in [(0, 1, 2)]:
+                accumulate(chosen, rest, False, degree)
+
+        def finish(degree):
+            for chosen in [(3, 4, 5), (6, 7, 8)]:
+                accumulate(chosen, rest, False, degree)
+
+        def turn_over(degree):
+            project(left_derivative, lead, moved)
+            if degree is not None:
+                finish(degree)
+            for chosen in []:
+                accumulate(chosen, lead, True)
+
+        def block(work):
+            def once(i, carry):
+                work()
+                return carry
+
+            lax.fori_loop(0, jnp.minimum(step + 1, 1), once, 0)
+
+        def one_degree(degree, carry):
+            block(lambda: first_part(degree))
+            block(lambda: turn_over(degree))
             return carry
 
-        lax.fori_loop(0, 2, two_degrees, 0)
-        degree_step(5, moved, None)
+        turn_over(None)
+        lax.fori_loop(1, ORDER - 1, one_degree, 0)
+        block(lambda: first_part(ORDER - 1))
+        finish(ORDER - 1)
 
         use_half = jnp.logical_or(cluster[...] == 1, step == 0)
         for q in range(VARS):
@@ -497,8 +528,10 @@
             for q in range(VARS):
                 term = aligned[q] * slot_rows[p, pl.ds(q, 1), :]
                 total = term if total is None else total + term
-            mixed[pl.ds(p * FPAD, FPAD), :] = total
-        scattered = two_dots(mixed[...], pick_ghost[...])
+            high, low = split(total)
+            mixed[pl.ds(p * FPAD, FPAD), pl.ds(0, SLOTS)] = high.astype(BF16)
+            mixed[pl.ds(p * FPAD, FPAD), pl.ds(SLOTS, SLOTS)] = low.astype(BF16)
+        scattered = dot(mixed[...], jnp.concatenate([pick_ghost[...]] * 2, axis=0))
         for p in range(VARS):
             tiles = [
                 scattered[p * FPAD : (p + 1) * FPAD, f * LANES : (f + 1) * LANES] for f in range(4)
@@ -573,7 +606,7 @@
             pltpu.VMEM((SLOTS, 4 * LANES), BF16),
             pltpu.VMEM((VARS, KDIM, LANES), BF16),
             pltpu.VMEM((3 * VARS, BASIS, LANES), F32),
-            pltpu.VMEM((3 * VARS, BASIS, LANES), F32),
+            pltpu.VMEM((VARS, BASIS, LANES), F32),
             pltpu.VMEM((VARS, BASIS, LANES), F32),
             pltpu.VMEM((VARS, BASIS, LANES), F32),
             pltpu.VMEM((ORDER, VARS, BASIS, LANES), F32),
@@ -581,7 +614,7 @@
             pltpu.VMEM((4 * VARS, FPAD, LANES), F32),
             pltpu.VMEM((2 * WIDE, 4 * LANES), BF16),
             pltpu.VMEM((VARS, 12 * FPAD, LANES), BF16),
-            pltpu.VMEM((ROWS, SLOTS), F32),
+            pltpu.VMEM((ROWS, 2 * SLOTS), BF16),
             pltpu.VMEM((2, 4 * PAIRS, LANES), F32),
             pltpu.VMEM((VARS, 16, SLOTS), F32),
             pltpu.VMEM((1, SLOTS), jnp.int32),

time: 32.1 us -> 31.9 us (level)
  no operation moved by 1% of the time
where the time goes in v4:
time: 31.9 us; the launch traced here: 31.7 us
  Pallas kernels  31 us (97%)
  local copies, waits for them, and re-layouts  0.7 us (2%)
    pallas_call x1, Pallas kernels, body(): pl.pallas_call(functools.partial(kernel, n_dom, n_sub, remote), name='ela...  31 us
    unnamed x1, local copies, waits for them, and re-layouts  0.7 us

profile of v4, /device:TPU:1, one launch (start us, length us, event | category | flops | bytes accessed | tf_op | source)
XLA Modules:
  0.0 31.7 jit_solution(17537158347464403858)
XLA Ops:
  0.0 31.0 %elastic_step.1 = f32[9,56,128]{2,1,0:T(8,128)S(1)} custom-call(f32[9,56,128]{2,1,0:T(8,128)} %bitcast.17, s32[1,128]{1,0:T(1,128)} %bitcast.24, s32[1,128]{1,0:T(1,128)} %bitcast.25, s32[4,128]{1,0:T(4,128)} %neighbour_hbm.1, s32[4,128]{1,0:T(4,128)} %flux_hbm.1, s32[1,192]{1,0:T(1,128)} %bitcast.23, f32[3,56,56]{2,1,0:T(8,128)} %derivative_hbm.1, ...), custom_call_target="tpu_custom_call" | custom-call | tf_op jit(solution)/shard_map/elastic_step/pallas_call | solution.py:582
  31.0 0.7 %copy.16 = f32[56,9,128]{2,0,1:T(8,128)} copy(f32[56,9,128]{2,0,1:T(8,128)S(1)} %bitcast.16) | data formatting | bytes 516096

commit v5 on v4

--- a/solution.py
+++ b/solution.py
@@ -111,6 +111,7 @@
     pick_ghost,
     current,
     moved,
+    moved_rest,
     partial,
     half_sum,
     late_sum,
@@ -326,7 +327,7 @@
             totals = [None] * len(chosen)
             for q in group:
                 for d in range(3):
-                    block = moved[d * VARS + q]
+                    block = (moved if q in lead else moved_rest)[d * VARS + q]
                     for i, p in enumerate(chosen):
                         term = block * star_rows[p, pl.ds(d * VARS + q, 1), :]
                         totals[i] = term if totals[i] is None else totals[i] + term
@@ -341,9 +342,9 @@
                     current[p] = right_operand(values, 8)
 
         def first_part(degree):
-            project(left_derivative, rest, moved)
             for chosen in [(0, 1, 2), (3, 4, 5), (6, 7, 8)]:
                 accumulate(chosen, lead, True)
+            project(left_derivative, rest, moved_rest)
             for chosen in [(0, 1, 2)]:
                 accumulate(chosen, rest, False, degree)
 
@@ -352,11 +353,11 @@
                 accumulate(chosen, rest, False, degree)
 
         def turn_over(degree):
+            if degree is not None:
+                accumulate((3, 4, 5), rest, False, degree)
             project(left_derivative, lead, moved)
             if degree is not None:
-                finish(degree)
-            for chosen in []:
-                accumulate(chosen, lead, True)
+                accumulate((6, 7, 8), rest, False, degree)
 
         def block(work):
             def once(i, carry):
@@ -606,6 +607,7 @@
             pltpu.VMEM((SLOTS, 4 * LANES), BF16),
             pltpu.VMEM((VARS, KDIM, LANES), BF16),
             pltpu.VMEM((3 * VARS, BASIS, LANES), F32),
+            pltpu.VMEM((3 * VARS, BASIS, LANES), F32),
             pltpu.VMEM((VARS, BASIS, LANES), F32),
             pltpu.VMEM((VARS, BASIS, LANES), F32),
             pltpu.VMEM((VARS, BASIS, LANES), F32),

time: 31.9 us -> 30.7 us (0.962)
  Pallas kernels: 31 us -> 29.9 us
    pallas_call x1, Pallas kernels: 31 us -> 29.9 us  [body(): pl.pallas_call(functools.partial(kernel, n_dom, n_sub, remote), name='ela...]
where the time goes in v5:
time: 30.7 us; the launch traced here: 30.6 us
  Pallas kernels  29.9 us (97%)
  local copies, waits for them, and re-layouts  0.7 us (2%)
    pallas_call x1, Pallas kernels, body(): pl.pallas_call(functools.partial(kernel, n_dom, n_sub, remote), name='ela...  29.9 us
    unnamed x1, local copies, waits for them, and re-layouts  0.7 us

profile of v5, /device:TPU:1, one launch (start us, length us, event | category | flops | bytes accessed | tf_op | source)
XLA Modules:
  0.0 30.6 jit_solution(5898242571161765768)
XLA Ops:
  0.0 29.9 %elastic_step.1 = f32[9,56,128]{2,1,0:T(8,128)S(1)} custom-call(f32[9,56,128]{2,1,0:T(8,128)} %bitcast.17, s32[1,128]{1,0:T(1,128)} %bitcast.24, s32[1,128]{1,0:T(1,128)} %bitcast.25, s32[4,128]{1,0:T(4,128)} %neighbour_hbm.1, s32[4,128]{1,0:T(4,128)} %flux_hbm.1, s32[1,192]{1,0:T(1,128)} %bitcast.23, f32[3,56,56]{2,1,0:T(8,128)} %derivative_hbm.1, ...), custom_call_target="tpu_custom_call" | custom-call | tf_op jit(solution)/shard_map/elastic_step/pallas_call | solution.py:583
  29.9 0.7 %copy.16 = f32[56,9,128]{2,0,1:T(8,128)} copy(f32[56,9,128]{2,0,1:T(8,128)S(1)} %bitcast.16) | data formatting | bytes 516096

commit v6 on v5

--- a/solution.py
+++ b/solution.py
@@ -317,7 +317,7 @@
         return value
 
     def phase(step, carry):
-        for q in range(VARS):
+        def begin(q):
             values = out[q]
             current[q] = right_operand(values, 8)
             half_sum[q] = values * half_weights[0]
@@ -371,7 +371,11 @@
             block(lambda: turn_over(degree))
             return carry
 
+        for q in range(6):
+            begin(q)
         turn_over(None)
+        for q in range(6, VARS):
+            begin(q)
         lax.fori_loop(1, ORDER - 1, one_degree, 0)
         block(lambda: first_part(ORDER - 1))
         finish(ORDER - 1)

time: 30.7 us -> 30.7 us (level)
  no operation moved by 1% of the time
where the time goes in v6:
time: 30.7 us; the launch traced here: 30.6 us
  Pallas kernels  29.9 us (97%)
  local copies, waits for them, and re-layouts  0.7 us (2%)
    pallas_call x1, Pallas kernels, body(): pl.pallas_call(functools.partial(kernel, n_dom, n_sub, remote), name='ela...  29.9 us
    unnamed x1, local copies, waits for them, and re-layouts  0.7 us

profile of v6, /device:TPU:1, one launch (start us, length us, event | category | flops | bytes accessed | tf_op | source)
XLA Modules:
  0.0 30.6 jit_solution(13040412537882230506)
XLA Ops:
  0.0 29.9 %elastic_step.1 = f32[9,56,128]{2,1,0:T(8,128)S(1)} custom-call(f32[9,56,128]{2,1,0:T(8,128)} %bitcast.17, s32[1,128]{1,0:T(1,128)} %bitcast.24, s32[1,128]{1,0:T(1,128)} %bitcast.25, s32[4,128]{1,0:T(4,128)} %neighbour_hbm.1, s32[4,128]{1,0:T(4,128)} %flux_hbm.1, s32[1,192]{1,0:T(1,128)} %bitcast.23, f32[3,56,56]{2,1,0:T(8,128)} %derivative_hbm.1, ...), custom_call_target="tpu_custom_call" | custom-call | tf_op jit(solution)/shard_map/elastic_step/pallas_call | solution.py:587
  29.9 0.7 %copy.16 = f32[56,9,128]{2,0,1:T(8,128)} copy(f32[56,9,128]{2,0,1:T(8,128)S(1)} %bitcast.16) | data formatting | bytes 516096
